TPU v7x, 128 devices: a whole 4x4x4 slice. The times are simulated.
128 devices in a mesh: sa: 4 (over x), sb: 2 (over core), sc: 16 (over z, y).
Axes of the slice: x: 4, y: 4, z: 4, core: 2. Of those that a mesh axis runs over, the one named last changes fastest.
Arguments:
- queries: float32 [65536, 2048], P(('sa', 'sb', 'sc')), may hold values from -6 to 6
- key_rows: float32 [65536, 2048], P(('sa', 'sb', 'sc')), may hold values from -6 to 6
- value_rows: float32 [65536, 2048], P(('sa', 'sb', 'sc')), may hold values from -6 to 6
- out_grad: float32 [65536, 2048], P(('sa', 'sb', 'sc')), may hold values from -6 to 6
- prefix_state: float32 [16, 128, 128], replicated, may hold values from -1536 to 1536
- suffix_state: float32 [16, 128, 128], replicated, may hold values from -1536 to 1536
Outputs:
- query_grad: bfloat16 [65536, 2048], P(('sa', 'sb', 'sc'))
- key_grad: bfloat16 [65536, 2048], P(('sa', 'sb', 'sc'))
- value_grad: bfloat16 [65536, 2048], P(('sa', 'sb', 'sc'))
All inputs are finite; a program needn't handle non-finite values.
Results may differ from a plain program's by a relative error of at most 0.0019.
Values sent between devices are 32-bit elements; how exact they have to be, the bound alone decides.
A program may use at most 576 MiB of HBM per device.

v0:
```python
import math

import jax
import jax.numpy as jnp
from jax import lax
from jax.sharding import PartitionSpec as P


def entering(part, axis, combine, identity):
    place = lax.axis_index(axis)
    gathered = jax.tree.map(lambda a: lax.all_gather(a, axis), part)
    state = jax.tree.map(lambda a, e: jnp.zeros_like(a) + jnp.asarray(e, a.dtype), part, identity)

    def one(hop, state):
        return combine(
            state, jax.tree.map(lambda a: lax.dynamic_index_in_dim(a, hop, 0, False), gathered)
        )

    return lax.fori_loop(0, place, one, state)


def add_states(earlier, later):
    return jax.tree.map(lambda left, right: left + right, earlier, later)


def run_chain(local_terms):
    zero_state = jax.tree.map(jnp.zeros_like, local_terms)
    inner_part = entering(local_terms, "sc", add_states, zero_state)
    group_sum = lax.psum((local_terms[0], local_terms[1]), "sc")
    middle_part = entering(group_sum, "sb", add_states, zero_state)
    block_sum = lax.psum((group_sum[0], group_sum[1]), "sb")
    outer_part = entering(block_sum, "sa", add_states, zero_state)
    return add_states(add_states(outer_part, middle_part), inner_part)


def shards(queries, key_rows, value_rows, out_grad, prefix_state, suffix_state):
    row_count = queries.shape[0]
    head_count = prefix_state.shape[0]
    head_size = prefix_state.shape[1]
    device_count = lax.axis_size("sa") * lax.axis_size("sb") * lax.axis_size("sc")
    factor = 1.0 / math.sqrt(head_size * row_count * device_count)
    highest = lax.Precision.HIGHEST
    shaped = (row_count, head_count, head_size)
    query_t = queries.reshape(shaped)
    key_t = key_rows.reshape(shaped)
    value_t = value_rows.reshape(shaped)
    grad_t = out_grad.reshape(shaped)
    kv_local = jnp.einsum("thd,the->hde", key_t, value_t, precision=highest)
    grad_local = jnp.einsum("the,thd->hed", grad_t, query_t, precision=highest)
    prior_kv, prior_grad = run_chain((kv_local, grad_local))
    total_grad = lax.psum(grad_local, ("sa", "sb", "sc"))
    state_before = prefix_state + prior_kv
    state_after = suffix_state + (total_grad - prior_grad - grad_local)
    lower = (
        lax.broadcasted_iota(jnp.int32, (row_count, row_count), 0)
        >= lax.broadcasted_iota(jnp.int32, (row_count, row_count), 1)
    ).astype(jnp.float32)
    grad_scores = jnp.einsum("the,she->hts", grad_t, value_t, precision=highest) * lower
    attn_scores = jnp.einsum("thd,shd->hts", query_t, key_t, precision=highest) * lower
    query_grad = factor * (
        jnp.einsum("the,hde->thd", grad_t, state_before, precision=highest)
        + jnp.einsum("hts,shd->thd", grad_scores, key_t, precision=highest)
    )
    key_grad = factor * (
        jnp.einsum("she,hed->shd", value_t, state_after, precision=highest)
        + jnp.einsum("hts,thd->shd", grad_scores, query_t, precision=highest)
    )
    value_grad = factor * (
        jnp.einsum("shd,hed->she", key_t, state_after, precision=highest)
        + jnp.einsum("hts,the->she", attn_scores, grad_t, precision=highest)
    )
    flat = (row_count, head_count * head_size)
    return (
        query_grad.astype(jnp.bfloat16).reshape(flat),
        key_grad.astype(jnp.bfloat16).reshape(flat),
        value_grad.astype(jnp.bfloat16).reshape(flat),
    )


def solution(mesh):
    return jax.shard_map(
        shards,
        mesh=mesh,
        in_specs=(
            P(("sa", "sb", "sc"), None),
            P(("sa", "sb", "sc"), None),
            P(("sa", "sb", "sc"), None),
            P(("sa", "sb", "sc"), None),
            P(),
            P(),
        ),
        out_specs=(
            P(("sa", "sb", "sc"), None),
            P(("sa", "sb", "sc"), None),
            P(("sa", "sb", "sc"), None),
        ),
        check_vma=False,
    )
```

profile of v0, /device:TPU:1, one launch (start us, length us, event | category | flops | bytes accessed | tf_op | source)
XLA Modules:
  0.0 613.8 jit_solution(8954921210702635121)
XLA Ops:
  8.0 11.2 %fusion.21 = f32[16,128,128]{2,1,0:T(8,128)} fusion(f32[512,2048]{1,0:T(8,128)} %param.14, f32[512,2048]{1,0:T(8,128)} %param.13), kind=kOutput, calls=%fused_computation.27 | convolution fusion | flops 1610612736 | bytes 9437184 | tf_op jit(solution)/shard_map/thd,the->hde/dot_general | solution.py:48
  19.2 5.1 copy.46
  24.3 5.8 copy.27
  30.1 9.2 %fusion.16 = f32[16,128,128]{2,1,0:T(8,128)} fusion(f32[512,16,128]{0,2,1:T(8,128)} %copy.27, f32[512,2048]{1,0:T(8,128)} %param.12), kind=kOutput, calls=%fused_computation.22 | convolution fusion | flops 1610612736 | bytes 9437184 | tf_op jit(solution)/shard_map/the,thd->hed/dot_general | solution.py:49
  39.3 94.7 %all-gather.19.cloned.1.call-done = f32[256,128,128]{2,1,0:T(8,128)} async-done(((f32[16,128,128]{2,1,0:T(8,128)}), f32[256,128,128]{2,1,0:T(8,128)}) %all-gather.19.cloned.1.call-update) | async-done | bytes 16777232 | tf_op jit(solution)/shard_map/all_gather | solution.py:11
  134.8 93.1 %all-reduce.8.cloned.1.call-done = (f32[16,128,128]{2,1,0:T(8,128)}, f32[16,128,128]{2,1,0:T(8,128)}) async-done(((f32[16,128,128]{2,1,0:T(8,128)}, f32[16,128,128]{2,1,0:T(8,128)}), (f32[16,128,128]{2,1,0:T(8,128)}, f32[16,128,128]{2,1,0:T(8,128)})) %all-reduce.8.cloned.1.call-update) | async-done | bytes 2097168 | tf_op jit(solution)/shard_map/psum | solution.py:29
  228.5 15.4 %all-gather.15.cloned.1.call-done = f32[32,128,128]{2,1,0:T(8,128)} async-done(((f32[16,128,128]{2,1,0:T(8,128)}), f32[32,128,128]{2,1,0:T(8,128)}) %all-gather.15.cloned.1.call-update) | async-done | bytes 2097168 | tf_op jit(solution)/shard_map/all_gather | solution.py:11
  243.9 16.3 %all-gather.17.cloned.1.call-done = f32[32,128,128]{2,1,0:T(8,128)} async-done(((f32[16,128,128]{2,1,0:T(8,128)}), f32[32,128,128]{2,1,0:T(8,128)}) %all-gather.17.cloned.1.call-update) | async-done | bytes 2097168 | tf_op jit(solution)/shard_map/all_gather | solution.py:11
  261.4 30.2 %all-reduce.10.cloned.1.call-done = (f32[1,16,128,128]{3,2,1,0:T(8,128)}, f32[1,16,128,128]{3,2,1,0:T(8,128)}) async-done(((f32[1,16,128,128]{3,2,1,0:T(8,128)}, f32[1,16,128,128]{3,2,1,0:T(8,128)}), (f32[1,16,128,128]{3,2,1,0:T(8,128)}, f32[1,16,128,128]{3,2,1,0:T(8,128)})) %all-reduce.10.cloned.1.call-update) | async-done | bytes 2097168 | tf_op jit(solution)/shard_map/psum | solution.py:31
  293.1 19.5 %fusion.14 = f32[16,512,512]{2,1,0:T(8,128)} fusion(f32[512,2048]{1,0:T(8,128)} %param.12, f32[512,2048]{1,0:T(8,128)} %param.13), kind=kOutput, calls=%fused_computation.20 | convolution fusion | flops 6442450944 | bytes 25165824 | tf_op jit(solution)/shard_map/thd,shd->hts/dot_general | solution.py:59
  312.6 14.5 %fusion.11 = f32[16,512,512]{2,1,0:T(8,128)S(1)} fusion(f32[512,2048]{1,0:T(8,128)S(1)} %copy-done.4, f32[512,2048]{1,0:T(8,128)S(1)} %copy-done.5), kind=kOutput, calls=%fused_computation.17 | convolution fusion | flops 6442450944 | bytes 25165824 | tf_op jit(solution)/shard_map/the,she->hts/dot_general | solution.py:58
  327.1 14.5 %fusion.2 = f32[16,512,128]{1,2,0:T(8,128)} fusion(f32[16,512,512]{2,1,0:T(8,128)S(1)} %fusion.11, f32[512,512]{1,0:T(8,128)S(1)} %fusion.55, f32[512,2048]{1,0:T(8,128)} %param.12), kind=kOutput, calls=%fused_computation.8 | convolution fusion | flops 6446645248 | bytes 26214400 | tf_op jit(solution)/shard_map/hts,thd->shd/dot_general | solution.py:66
  341.6 21.3 %fusion.4 = f32[16,512,128]{1,2,0:T(8,128)} fusion(f32[16,512,512]{2,1,0:T(8,128)S(1)} %fusion.11, f32[512,512]{1,0:T(8,128)S(1)} %fusion.55, f32[512,2048]{1,0:T(8,128)} %param.13), kind=kOutput, calls=%fused_computation.10 | convolution fusion | flops 6446645248 | bytes 26214400 | tf_op jit(solution)/shard_map/hts,shd->thd/dot_general | solution.py:62
  362.9 44.5 %all-gather.21.cloned.1.call-done = f32[256,128,128]{2,1,0:T(8,128)} async-done(((f32[16,128,128]{2,1,0:T(8,128)}), f32[256,128,128]{2,1,0:T(8,128)}) %all-gather.21.cloned.1.call-update) | async-done | bytes 16777232 | tf_op jit(solution)/shard_map/all_gather | solution.py:11
  410.9 45.8 %all-gather.11.cloned.1.call-done = f32[4,16,128,128]{3,2,1,0:T(8,128)} async-done(((f32[1,16,128,128]{3,2,1,0:T(8,128)}), f32[4,16,128,128]{3,2,1,0:T(8,128)}) %all-gather.11.cloned.1.call-update) | async-done | bytes 4194320 | tf_op jit(solution)/shard_map/all_gather | solution.py:11
  456.7 50.5 %all-gather.13.cloned.1.call-done = f32[4,16,128,128]{3,2,1,0:T(8,128)} async-done(((f32[1,16,128,128]{3,2,1,0:T(8,128)}), f32[4,16,128,128]{3,2,1,0:T(8,128)}) %all-gather.13.cloned.1.call-update) | async-done | bytes 4194320 | tf_op jit(solution)/shard_map/all_gather | solution.py:11
  508.4 44.6 %all-reduce.6.cloned.1.call-done = f32[16,128,128]{2,1,0:T(8,128)} async-done(((f32[16,128,128]{2,1,0:T(8,128)}), f32[16,128,128]{2,1,0:T(8,128)}) %all-reduce.6.cloned.1.call-update) | async-done | bytes 1048592 | tf_op jit(solution)/shard_map/psum | solution.py:51
  557.5 3.8 fusion.23
  561.3 14.6 %fusion.29 = bf16[512,16,128]{0,2,1:T(8,128)(2,1)} fusion(f32[16,128,512]{2,1,0:T(8,128)S(1)} %fusion.23, f32[512,16,128]{0,2,1:T(8,128)S(1)} %copy-done.3, f32[16,512,512]{2,1,0:T(8,128)} %fusion.14, f32[512,512]{1,0:T(8,128)S(1)} %copy-done.7), kind=kOutput, calls=%fused_computation.36 | convolution fusion | flops 6449790976 | bytes 28311552 | tf_op jit(solution)/shard_map/hts,the->she/dot_general | solution.py:70
  575.9 3.9 copy.40
  579.8 9.2 %fusion.31 = bf16[512,16,128]{0,2,1:T(8,128)(2,1)} fusion(f32[16,512,128]{1,2,0:T(8,128)} %fusion.2, f32[16,128,128]{2,1,0:T(8,128)} %copy-done.8, f32[512,2048]{1,0:T(8,128)} %param.14), kind=kOutput, calls=%fused_computation.39 | convolution fusion | flops 1613758464 | bytes 11534336 | tf_op jit(solution)/shard_map/she,hed->shd/dot_general | solution.py:65
  589.0 4.1 copy.39
  593.1 9.2 %fusion.33 = bf16[512,16,128]{0,2,1:T(8,128)(2,1)} fusion(f32[16,512,128]{1,2,0:T(8,128)} %fusion.4, f32[16,128,128]{2,1,0:T(8,128)} %param.16, f32[16,128,128]{2,1,0:T(8,128)S(1)} %get-tuple-element.107, f32[16,128,128]{2,1,0:T(8,128)S(1)} %get-tuple-element.105, f32[16,128,128]{2,1,0:T(8,128)S(1)} %get-tuple-element.106, f32[512,2048]{1,0:T(8,128)} %param.15), kind=kOutput, calls=%fused_computation.42 | convolution fusion | flops 1614544896 | bytes 14680064 | tf_op jit(solution)/shard_map/the,hde->thd/dot_general | solution.py:61
  602.3 3.9 copy.38
  (48 shorter events, 15.3 us)
Async XLA Ops:
  8.0 126.0 %all-gather.19.cloned.1.call-start = ((), (), s32[]{:S(2)}) async-start(), calls=%async_computation.5 | async-start | bytes 17825792 | tf_op jit(solution)/shard_map/all_gather | solution.py:11
  134.0 93.9 %all-reduce.8.cloned.1.call-start = ((), (), s32[]{:S(2)}) async-start(), calls=%async_computation.7 | async-start | bytes 4194304 | tf_op jit(solution)/shard_map/psum | solution.py:29
  134.8 109.2 %all-gather.15.cloned.1.call-start = ((), (), s32[]{:S(2)}) async-start(), calls=%async_computation.3 | async-start | bytes 3145728 | tf_op jit(solution)/shard_map/all_gather | solution.py:11
  228.0 32.2 %all-gather.17.cloned.1.call-start = ((), (), s32[]{:S(2)}) async-start(), calls=%async_computation.4 | async-start | bytes 3145728 | tf_op jit(solution)/shard_map/all_gather | solution.py:11
  260.2 31.4 %all-reduce.10.cloned.1.call-start = ((), (), s32[]{:S(2)}) async-start(), calls=%async_computation.8 | async-start | bytes 4194304 | tf_op jit(solution)/shard_map/psum | solution.py:31
  260.8 146.6 %all-gather.21.cloned.1.call-start = ((), (), s32[]{:S(2)}) async-start(), calls=%async_computation.6 | async-start | bytes 17825792 | tf_op jit(solution)/shard_map/all_gather | solution.py:11
  261.4 195.3 %all-gather.11.cloned.1.call-start = ((), (), s32[]{:S(2)}) async-start(), calls=%async_computation | async-start | bytes 5242880 | tf_op jit(solution)/shard_map/all_gather | solution.py:11
  291.6 215.6 %all-gather.13.cloned.1.call-start = ((), (), s32[]{:S(2)}) async-start(), calls=%async_computation.1 | async-start | bytes 5242880 | tf_op jit(solution)/shard_map/all_gather | solution.py:11
  292.3 260.6 %all-reduce.6.cloned.1.call-start = ((), (), s32[]{:S(2)}) async-start(), calls=%async_computation.2 | async-start | bytes 2097152 | tf_op jit(solution)/shard_map/psum | solution.py:51
  293.0 48.6 %copy-start.6 = (f32[512,512]{1,0:T(8,128)}, f32[512,512]{1,0:T(8,128)S(1)}, u32[]{:S(2)}) copy-start(f32[512,512]{1,0:T(8,128)S(1)} %fusion.55) | copy-start | bytes 3145732
  293.1 19.6 %copy-start.4 = (f32[512,2048]{1,0:T(8,128)S(1)}, f32[512,2048]{1,0:T(8,128)}, u32[]{:S(2)}) copy-start(f32[512,2048]{1,0:T(8,128)} %param.15) | copy-start | bytes 12582916
  293.1 19.6 %copy-start.5 = (f32[512,2048]{1,0:T(8,128)S(1)}, f32[512,2048]{1,0:T(8,128)}, u32[]{:S(2)}) copy-start(f32[512,2048]{1,0:T(8,128)} %param.14) | copy-start | bytes 12582916
  407.6 1.0 copy-start.1
  410.9 45.8 %copy-start.2 = (f32[16,128,128]{2,1,0:T(8,128)}, f32[16,128,128]{2,1,0:T(8,128)S(1)}, u32[]{:S(2)}) copy-start(f32[16,128,128]{2,1,0:T(8,128)S(1)} %get-tuple-element.109) | copy-start | bytes 3145732
  552.9 4.5 copy-start
  556.4 1.0 copy-start.8
  557.5 3.8 copy-start.3
  557.5 3.8 copy-start.7
Sparse Core Ops, SparseCore 0:
  19.4 114.6 all-gather.18
  138.8 89.0 all-reduce.7
  229.7 14.2 all-gather.14
  245.5 14.6 all-gather.16
  263.4 28.1 all-reduce.9
  294.1 113.1 all-gather.20
  409.0 47.6 all-gather.10
  458.3 48.7 all-gather.12
Sparse Core Ops, SparseCore 1:
  298.2 254.7 all-reduce.5
where the time goes:
time: 621 us; the launch traced here: 614 us
  waiting for transfers between devices  439 us (71%)
  matrix products  127 us (20%)
  local copies, waits for them, and re-layouts  26.3 us (4%)
  between operations  16 us (3%)
    all_gather x6, waiting for transfers between devices, entering(): gathered = jax.tree.map(lambda a: lax.all_gather(a, axis), part)  267 us
    psum x1, waiting for transfers between devices, run_chain(): group_sum = lax.psum((local_terms[0], local_terms[1]), 'sc')  93.1 us
    psum x1, waiting for transfers between devices, shards(): total_grad = lax.psum(grad_local, ('sa', 'sb', 'sc'))  44.6 us
    psum x1, waiting for transfers between devices, run_chain(): block_sum = lax.psum((group_sum[0], group_sum[1]), 'sb')  30.2 us
    dot_general x1, matrix products, shards(): jnp.einsum('hts,shd->thd', grad_scores, key_t, precision=highest)  21.3 us
    dot_general x1, matrix products, shards(): jnp.einsum('thd,shd->hts', query_t, key_t, precision=highest) * lower  19.5 us
    unnamed x22, local copies, waits for them, and re-layouts  19 us
    dot_general x1, matrix products, shards(): jnp.einsum('hts,the->she', attn_scores, grad_t, precision=highest)  14.6 us
  transfers between devices with their start and end apart: 9, of which 9 were waited for; matrix products, arithmetic and copies ran while one was open for 15% of the time, Pallas kernels for 0%

commit v1 on v0

v1 whole, which is shorter than its diff:
```python
import functools
import math

import jax
import jax.numpy as jnp
from jax import lax
from jax.experimental import pallas as pl
from jax.experimental.pallas import tpu as pltpu
from jax.sharding import PartitionSpec as P

MESH = pl.DeviceIdType.MESH
F32 = jnp.float32
BF16 = jnp.bfloat16
SEGMENTS = (4, 4, 4, 4)


def split2(x):
    hi = x.astype(BF16)
    lo = (x - hi.astype(F32)).astype(BF16)
    return jnp.concatenate([hi, lo], axis=1)


def halves(x):
    hi = x.astype(BF16)
    lo = (x - hi.astype(F32)).astype(BF16)
    return hi, lo


def mm(a, b):
    return jnp.dot(a, b, preferred_element_type=F32)


def mm_nt(a, b):
    return lax.dot_general(a, b, (((1,), (1,)), ((), ())), preferred_element_type=F32)


def fold_columns(r):
    n = r.shape[1] // 2
    return r[:, :n] + r[:, n:]


def fold_rows(r):
    n = r.shape[0] // 2
    return r[:n] + r[n:]


def scores(a2, b2):
    e = a2.shape[1] // 2
    swapped = jnp.concatenate([b2[:, e:], b2[:, :e]], axis=1)
    return mm_nt(
        jnp.concatenate([a2, a2], axis=1), jnp.concatenate([b2, swapped], axis=1)
    )


def kernel(
    axes, factor,
    q_hbm, k_hbm, v_hbm, g_hbm, prefix_hbm, suffix_hbm,
    qg_hbm, kg_hbm, vg_hbm,
    q2, k2, v2, g2, qt, gt, acc_q, acc_k, acc_v, land_q,
    local, gathered, totals, entering, ends, stage,
    load_sem, end_sem, in_send, in_recv, tot_send, tot_recv, out_send, out_recv, store_sem,
):
    nx, nc, ns = axes
    groups = nx * nc
    sa, sb, sc = lax.axis_index("sa"), lax.axis_index("sb"), lax.axis_index("sc")
    group = sa * nc + sb
    heads, rows, e = acc_q.shape
    half = rows // 2

    def peer(j):
        return (sa, sb, j)

    def group_peer(g):
        return (g // nc, lax.rem(g, nc), sc)

    landing = ((k_hbm, acc_q), (v_hbm, acc_k), (g_hbm, acc_v), (q_hbm, land_q))

    def load(a, h):
        src, dst = landing[a]
        return pltpu.make_async_copy(
            src.at[:, pl.ds(pl.multiple_of(h * e, e), e)], dst.at[h], load_sem.at[a, h]
        )

    def head_at(i):
        return lax.rem(sc + 1 + i, ns)

    for pair in ((0, 1), (2, 3)):
        @pl.loop(0, heads)
        def _(i):
            for a in pair:
                load(a, head_at(i)).start()

    end_copies = [
        pltpu.make_async_copy(prefix_hbm.at[sc], ends.at[0], end_sem.at[0]),
        pltpu.make_async_copy(suffix_hbm.at[sc], ends.at[1], end_sem.at[1]),
    ]
    for c in end_copies:
        c.start()

    barrier = pltpu.get_barrier_semaphore()

    @pl.loop(1, ns)
    def _(i):
        pl.semaphore_signal(barrier, inc=1, device_id=peer(lax.rem(sc + i, ns)), device_id_type=MESH)

    @pl.loop(1, groups)
    def _(i):
        pl.semaphore_signal(barrier, inc=1, device_id=group_peer(lax.rem(group + i, groups)), device_id_type=MESH)

    pl.semaphore_wait(barrier, ns - 1 + groups - 1)

    def in_copy(w, head, source, target):
        return pltpu.make_async_remote_copy(
            src_ref=local.at[w, head], dst_ref=gathered.at[w, source],
            send_sem=in_send.at[w, head], recv_sem=in_recv.at[w, source],
            device_id=peer(target), device_id_type=MESH,
        )

    def total_copy(w, source, target):
        return pltpu.make_async_remote_copy(
            src_ref=totals.at[w, source], dst_ref=totals.at[w, source],
            send_sem=tot_send.at[w, target], recv_sem=tot_recv.at[w, source],
            device_id=group_peer(target), device_id_type=MESH,
        )

    def out_copy(w, head, target):
        return pltpu.make_async_remote_copy(
            src_ref=gathered.at[w, target], dst_ref=entering.at[w, head],
            send_sem=out_send.at[w, target], recv_sem=out_recv.at[w, head],
            device_id=peer(target), device_id_type=MESH,
        )

    def local_sum(w, left, right, left_t, left2, right2):
        @pl.loop(0, heads)
        def _(i):
            h = head_at(i)
            a, b = left, right
            load(a, h).wait()
            load(b, h).wait()
            x2 = split2(landing[a][1][h])
            y2 = split2(landing[b][1][h])
            left2[h] = x2
            right2[h] = y2
            xt = x2.T
            if left_t is not None:
                left_t[h] = xt
            local[w, h] = fold_columns(fold_rows(mm(xt, y2)))

            @pl.when(h != sc)
            def _():
                in_copy(w, h, sc, h).start()

    local_sum(0, 1, 0, None, v2, k2)
    local_sum(1, 2, 3, gt, g2, q2)

    lower = lax.broadcasted_iota(jnp.int32, (half, half), 0) >= lax.broadcasted_iota(
        jnp.int32, (half, half), 1
    )

    def within_block(h):
        qt[h] = q2[h].T
        top, low = pl.ds(0, half), pl.ds(half, half)

        def three(a2, b2):
            s00 = jnp.where(lower, scores(a2[h, top, :], b2[h, top, :]), 0.0)
            s10 = scores(a2[h, low, :], b2[h, top, :])
            s11 = jnp.where(lower, scores(a2[h, low, :], b2[h, low, :]), 0.0)
            return halves(s00), halves(s10), halves(s11)

        def transposed(xt, parts):
            (h00, l00), (h10, l10), (h11, l11) = parts
            x = xt[h]
            first = mm(
                jnp.concatenate([x, x], axis=1),
                jnp.concatenate([h00, h10, l00, l10], axis=0),
            )
            y = x[:, half:]
            second = mm(
                jnp.concatenate([y, y], axis=1), jnp.concatenate([h11, l11], axis=0)
            )
            return fold_rows(first).T, fold_rows(second).T

        parts = three(g2, v2)
        (h00, l00), (h10, l10), (h11, l11) = parts
        kk = k2[h]
        acc_q[h, top, :] = fold_columns(
            fold_rows(mm(jnp.concatenate([h00, l00], axis=0), kk[:half]))
        )
        wide = jnp.concatenate(
            [jnp.concatenate([h10, h11], axis=1), jnp.concatenate([l10, l11], axis=1)],
            axis=0,
        )
        acc_q[h, low, :] = fold_columns(fold_rows(mm(wide, kk)))
        first, second = transposed(qt, parts)
        acc_k[h, top, :] = first
        acc_k[h, low, :] = second
        first, second = transposed(gt, three(q2, k2))
        acc_v[h, top, :] = first
        acc_v[h, low, :] = second

    def segment(start, count):
        @pl.loop(start, start + count)
        def _(h):
            within_block(h)

    def send_totals(w):
        gathered[w, sc] = local[w, sc]

        @pl.loop(1, ns)
        def _(i):
            j = lax.rem(sc + i, ns)
            in_copy(w, j, j, j).wait_recv()

        total = gathered[w, 0]
        for j in range(1, ns):
            total = total + gathered[w, j]
        totals[w, group] = total

        @pl.loop(1, groups)
        def _(i):
            total_copy(w, group, lax.rem(group + i, groups)).start()

    def send_states(w):
        @pl.loop(1, groups)
        def _(i):
            g = lax.rem(group + i, groups)
            total_copy(w, g, g).wait_recv()

        end_copies[w].wait()
        state = ends[w]
        if w == 0:
            state = state.T
        for g in range(groups):
            use = g < group if w == 0 else g > group
            state = state + jnp.where(use, totals[w, g], 0.0)
        for j in range(ns) if w == 0 else reversed(range(ns)):
            term = gathered[w, j]
            gathered[w, j] = state
            state = state + term
        entering[w, sc] = gathered[w, sc]

        @pl.loop(1, ns)
        def _(i):
            out_copy(w, sc, lax.rem(sc + i, ns)).start()

    done = 0
    for count, step in zip(
        SEGMENTS,
        (
            functools.partial(send_totals, 0),
            functools.partial(send_states, 0),
            functools.partial(send_totals, 1),
            functools.partial(send_states, 1),
        ),
    ):
        segment(done, count)
        done += count
        step()

    def store(o, h):
        dst = (qg_hbm, kg_hbm, vg_hbm)[o]
        return pltpu.make_async_copy(
            stage.at[o, h], dst.at[:, pl.ds(pl.multiple_of(h * e, e), e)], store_sem.at[o, h]
        )

    def finish(o, h, x2, acc, state):
        s2 = split2(state)
        r = fold_columns(mm(x2[h], jnp.concatenate([s2, s2], axis=0)))
        stage[o, h] = ((r + acc[h]) * factor).astype(BF16)
        store(o, h).start()

    def arrived(w, i):
        h = lax.rem(sc - i + ns, ns)

        @pl.when(i > 0)
        def _():
            out_copy(w, h, h).wait_recv()

        return h

    @pl.loop(0, heads)
    def _(i):
        h = arrived(0, i)
        finish(0, h, g2, acc_q, entering[0, h])

    @pl.loop(0, heads)
    def _(i):
        h = arrived(1, i)
        state = entering[1, h]
        finish(1, h, v2, acc_k, state)
        finish(2, h, k2, acc_v, state.T)

    for w in range(2):
        @pl.loop(1, ns)
        def _(i):
            j = lax.rem(sc + i, ns)
            in_copy(w, j, sc, j).wait_send()
            out_copy(w, sc, j).wait_send()

        @pl.loop(1, groups)
        def _(i):
            total_copy(w, group, lax.rem(group + i, groups)).wait_send()

    @pl.loop(0, heads)
    def _(h):
        for o in range(3):
            store(o, h).wait()


def shards(axes, queries, key_rows, value_rows, out_grad, prefix_state, suffix_state):
    rows = queries.shape[0]
    heads, e, _ = prefix_state.shape
    nx, nc, ns = axes
    groups = nx * nc
    factor = 1.0 / math.sqrt(e * rows * groups * ns)
    hbm = pl.BlockSpec(memory_space=pl.ANY)
    dma = pltpu.SemaphoreType.DMA
    out = jax.ShapeDtypeStruct((rows, heads * e), BF16)
    pair = pltpu.VMEM((heads, rows, 2 * e), BF16)
    pair_t = pltpu.VMEM((heads, 2 * e, rows), BF16)
    wide = pltpu.VMEM((heads, rows, e), F32)
    states = pltpu.VMEM((2, heads, e, e), F32)
    return pl.pallas_call(
        functools.partial(kernel, axes, factor),
        out_shape=(out, out, out),
        in_specs=[hbm] * 6,
        out_specs=(hbm, hbm, hbm),
        scratch_shapes=[
            pair, pair, pair, pair, pair_t, pair_t,
            wide, wide, wide, wide,
            states, states, pltpu.VMEM((2, groups, e, e), F32), states,
            pltpu.VMEM((2, e, e), F32),
            pltpu.VMEM((3, heads, rows, e), BF16),
            dma((4, heads)), dma((2,)),
            dma((2, ns)), dma((2, ns)),
            dma((2, groups)), dma((2, groups)),
            dma((2, ns)), dma((2, ns)),
            dma((3, heads)),
        ],
        compiler_params=pltpu.CompilerParams(
            collective_id=0, has_side_effects=True, vmem_limit_bytes=60 << 20
        ),
    )(queries, key_rows, value_rows, out_grad, prefix_state, suffix_state)


def solution(mesh):
    axes = tuple(mesh.shape[name] for name in ("sa", "sb", "sc"))
    split = P(("sa", "sb", "sc"), None)
    return jax.shard_map(
        functools.partial(shards, axes),
        mesh=mesh,
        in_specs=(split, split, split, split, P(), P()),
        out_specs=(split, split, split),
        check_vma=False,
    )
```

time: 621 us -> 75.9 us (0.12); the launches traced: 614 us -> 75.7 us
  waiting for transfers between devices: 439 us -> 0 us
  matrix products: 127 us -> 0 us
  Pallas kernels: 0 us -> 68.1 us
  local copies, waits for them, and re-layouts: 26.3 us -> 6.98 us
  between operations: 16 us -> 0.65 us
    all_gather x6 -> x0, waiting for transfers between devices: 267 us -> none  [entering(): gathered = jax.tree.map(lambda a: lax.all_gather(a, axis), part)]
    psum x3 -> x0, waiting for transfers between devices: 168 us -> none  [the longest x1 93.1 us: run_chain(): group_sum = lax.psum((local_terms[0], local_terms[1]), 'sc')]
    dot_general x10 -> x0, matrix products: 127 us -> none  [the longest x1 21.3 us: shards(): jnp.einsum('hts,shd->thd', grad_scores, key_t, precision=highest)]
    pallas_call x0 -> x1, Pallas kernels: none -> 68.1 us  [shards(): pl.pallas_call(functools.partial(kernel, axes, factor), out_shape=(out, o...]
    unnamed x22 -> x7, local copies, waits for them, and re-layouts: 19 us -> 6.98 us
  transfers between devices with their start and end apart: 9 -> 0, of which waited for: 9 -> 0; matrix products, arithmetic and copies ran while one was open for 15% -> 0% of each run, Pallas kernels for 0% -> 0%
where the time goes in v1:
time: 75.9 us; the launch traced here: 75.7 us
  Pallas kernels  68.1 us (90%)
  local copies, waits for them, and re-layouts  6.98 us (9%)
    pallas_call x1, Pallas kernels, shards(): pl.pallas_call(functools.partial(kernel, axes, factor), out_shape=(out, o...  68.1 us
    unnamed x7, local copies, waits for them, and re-layouts  6.98 us

profile of v1, /device:TPU:1, one launch (start us, length us, event | category | flops | bytes accessed | tf_op | source)
XLA Modules:
  0.0 75.7 jit_solution(12287025666871506074)
XLA Ops:
  0.6 68.1 %shard_map.85 = (bf16[512,2048]{1,0:T(8,128)(2,1)}, bf16[512,2048]{1,0:T(8,128)(2,1)}, bf16[512,2048]{1,0:T(8,128)(2,1)}) custom-call(f32[512,2048]{1,0:T(8,128)} %q_hbm.1, f32[512,2048]{1,0:T(8,128)} %k_hbm.1, f32[512,2048]{1,0:T(8,128)} %v_hbm.1, f32[512,2048]{1,0:T(8,128)} %g_hbm.1, f32[16,128,128]{2,1,0:T(8,128)} %prefix_hbm.1, f32[16,128,128]{2,1,0:T(8,128)} %suffix_hbm.1), custom_call_target="tpu_custom_call" | custom-call | tf_op jit(solution)/shard_map/pallas_call | solution.py:323
  68.8 0.0 copy-start.1
  68.8 3.3 %copy.12 = bf16[512,2048]{1,0:T(8,128)(2,1)} copy(bf16[512,2048]{1,0:T(8,128)(2,1)} %get-tuple-element.6) | data formatting | bytes 4194304
  72.1 0.0 copy-done.1
  72.1 0.0 copy-start
  72.1 1.3 %copy.13 = bf16[512,2048]{1,0:T(8,128)(2,1)} copy(bf16[512,2048]{1,0:T(8,128)(2,1)S(1)} %copy-done.1) | data formatting | bytes 4194304
  73.4 1.0 %copy-done = bf16[512,2048]{1,0:T(8,128)(2,1)S(1)} copy-done((bf16[512,2048]{1,0:T(8,128)(2,1)S(1)}, bf16[512,2048]{1,0:T(8,128)(2,1)}, u32[]{:S(2)}) %copy-start) | copy-done | bytes 2097176
  74.4 1.3 %copy.14 = bf16[512,2048]{1,0:T(8,128)(2,1)} copy(bf16[512,2048]{1,0:T(8,128)(2,1)S(1)} %copy-done) | data formatting | bytes 4194304
Async XLA Ops:
  68.8 3.3 %copy-start.1 = (bf16[512,2048]{1,0:T(8,128)(2,1)S(1)}, bf16[512,2048]{1,0:T(8,128)(2,1)}, u32[]{:S(2)}) copy-start(bf16[512,2048]{1,0:T(8,128)(2,1)} %get-tuple-element.7) | copy-start | bytes 6291460
  72.1 2.3 %copy-start = (bf16[512,2048]{1,0:T(8,128)(2,1)S(1)}, bf16[512,2048]{1,0:T(8,128)(2,1)}, u32[]{:S(2)}) copy-start(bf16[512,2048]{1,0:T(8,128)(2,1)} %get-tuple-element.8) | copy-start | bytes 6291460

commit v2 on v1

--- a/solution.py
+++ b/solution.py
@@ -11,7 +11,7 @@
 MESH = pl.DeviceIdType.MESH
 F32 = jnp.float32
 BF16 = jnp.bfloat16
-SEGMENTS = (4, 4, 4, 4)
+SEGMENTS = (1, 2, 6, 1, 6)
 
 
 def split2(x):
@@ -52,13 +52,19 @@
     )
 
 
+def finish(factor, x2, acc, state):
+    s2 = split2(state)
+    r = fold_columns(mm(x2, jnp.concatenate([s2, s2], axis=0)))
+    return ((r + acc) * factor).astype(BF16)
+
+
 def kernel(
     axes, factor,
     q_hbm, k_hbm, v_hbm, g_hbm, prefix_hbm, suffix_hbm,
-    qg_hbm, kg_hbm, vg_hbm,
-    q2, k2, v2, g2, qt, gt, acc_q, acc_k, acc_v, land_q,
-    local, gathered, totals, entering, ends, stage,
-    load_sem, end_sem, in_send, in_recv, tot_send, tot_recv, out_send, out_recv, store_sem,
+    k2, v2, acc_k, acc_v, after, qg,
+    q2, g2, qt, gt, acc_q, land_q,
+    local, gathered, totals, before, ends,
+    load_sem, end_sem, in_send, in_recv, tot_send, tot_recv, out_send, out_recv,
 ):
     nx, nc, ns = axes
     groups = nx * nc
@@ -66,6 +72,7 @@
     group = sa * nc + sb
     heads, rows, e = acc_q.shape
     half = rows // 2
+    entering = (before, after)
 
     def peer(j):
         return (sa, sb, j)
@@ -125,7 +132,7 @@
 
     def out_copy(w, head, target):
         return pltpu.make_async_remote_copy(
-            src_ref=gathered.at[w, target], dst_ref=entering.at[w, head],
+            src_ref=gathered.at[w, target], dst_ref=entering[w].at[head],
             send_sem=out_send.at[w, target], recv_sem=out_recv.at[w, head],
             device_id=peer(target), device_id_type=MESH,
         )
@@ -146,9 +153,11 @@
                 left_t[h] = xt
             local[w, h] = fold_columns(fold_rows(mm(xt, y2)))
 
-            @pl.when(h != sc)
-            def _():
-                in_copy(w, h, sc, h).start()
+            if w == 0:
+
+                @pl.when(h != sc)
+                def _():
+                    in_copy(w, h, sc, h).start()
 
     local_sum(0, 1, 0, None, v2, k2)
     local_sum(1, 2, 3, gt, g2, q2)
@@ -199,9 +208,19 @@
         acc_v[h, low, :] = second
 
     def segment(start, count):
+        if count == 0:
+            return
+
         @pl.loop(start, start + count)
         def _(h):
             within_block(h)
+
+    def send_next():
+        @pl.loop(1, ns)
+        def _(i):
+            j = lax.rem(sc + i, ns)
+            in_copy(0, j, sc, j).wait_send()
+            in_copy(1, j, sc, j).start()
 
     def send_totals(w):
         gathered[w, sc] = local[w, sc]
@@ -237,7 +256,7 @@
             term = gathered[w, j]
             gathered[w, j] = state
             state = state + term
-        entering[w, sc] = gathered[w, sc]
+        entering[w][sc] = gathered[w, sc]
 
         @pl.loop(1, ns)
         def _(i):
@@ -247,6 +266,7 @@
     for count, step in zip(
         SEGMENTS,
         (
+            send_next,
             functools.partial(send_totals, 0),
             functools.partial(send_states, 0),
             functools.partial(send_totals, 1),
@@ -256,18 +276,7 @@
         segment(done, count)
         done += count
         step()
-
-    def store(o, h):
-        dst = (qg_hbm, kg_hbm, vg_hbm)[o]
-        return pltpu.make_async_copy(
-            stage.at[o, h], dst.at[:, pl.ds(pl.multiple_of(h * e, e), e)], store_sem.at[o, h]
-        )
-
-    def finish(o, h, x2, acc, state):
-        s2 = split2(state)
-        r = fold_columns(mm(x2[h], jnp.concatenate([s2, s2], axis=0)))
-        stage[o, h] = ((r + acc[h]) * factor).astype(BF16)
-        store(o, h).start()
+    segment(done, heads - done)
 
     def arrived(w, i):
         h = lax.rem(sc - i + ns, ns)
@@ -281,25 +290,43 @@
     @pl.loop(0, heads)
     def _(i):
         h = arrived(0, i)
-        finish(0, h, g2, acc_q, entering[0, h])
+        qg[h] = finish(factor, g2[h], acc_q[h], before[h])
 
     @pl.loop(0, heads)
     def _(i):
-        h = arrived(1, i)
-        state = entering[1, h]
-        finish(1, h, v2, acc_k, state)
-        finish(2, h, k2, acc_v, state.T)
+        arrived(1, i)
 
     for w in range(2):
         @pl.loop(1, ns)
         def _(i):
             j = lax.rem(sc + i, ns)
-            in_copy(w, j, sc, j).wait_send()
+            if w == 1:
+                in_copy(w, j, sc, j).wait_send()
             out_copy(w, sc, j).wait_send()
 
         @pl.loop(1, groups)
         def _(i):
             total_copy(w, group, lax.rem(group + i, groups)).wait_send()
+
+
+def closing_kernel(
+    factor, k2, v2, acc_k, acc_v, after, qg, qg_hbm, kg_hbm, vg_hbm, kg, vg, store_sem
+):
+    heads, _, e = qg.shape
+
+    def store(o, h):
+        src, dst = ((qg, qg_hbm), (kg, kg_hbm), (vg, vg_hbm))[o]
+        return pltpu.make_async_copy(
+            src.at[h], dst.at[:, pl.ds(pl.multiple_of(h * e, e), e)], store_sem.at[o, h]
+        )
+
+    @pl.loop(0, heads)
+    def _(h):
+        state = after[h]
+        kg[h] = finish(factor, v2[h], acc_k[h], state)
+        vg[h] = finish(factor, k2[h], acc_v[h], state.T)
+        for o in range(3):
+            store(o, h).start()
 
     @pl.loop(0, heads)
     def _(h):
@@ -314,33 +341,41 @@
     groups = nx * nc
     factor = 1.0 / math.sqrt(e * rows * groups * ns)
     hbm = pl.BlockSpec(memory_space=pl.ANY)
+    vmem = pl.BlockSpec(memory_space=pltpu.VMEM)
     dma = pltpu.SemaphoreType.DMA
-    out = jax.ShapeDtypeStruct((rows, heads * e), BF16)
     pair = pltpu.VMEM((heads, rows, 2 * e), BF16)
     pair_t = pltpu.VMEM((heads, 2 * e, rows), BF16)
     wide = pltpu.VMEM((heads, rows, e), F32)
+    one = pltpu.VMEM((heads, e, e), F32)
     states = pltpu.VMEM((2, heads, e, e), F32)
-    return pl.pallas_call(
+    narrow = pltpu.VMEM((heads, rows, e), BF16)
+    kept = pl.pallas_call(
         functools.partial(kernel, axes, factor),
-        out_shape=(out, out, out),
+        out_shape=(pair, pair, wide, wide, one, narrow),
         in_specs=[hbm] * 6,
-        out_specs=(hbm, hbm, hbm),
+        out_specs=(vmem,) * 6,
         scratch_shapes=[
-            pair, pair, pair, pair, pair_t, pair_t,
-            wide, wide, wide, wide,
-            states, states, pltpu.VMEM((2, groups, e, e), F32), states,
+            pair, pair, pair_t, pair_t, wide, wide,
+            states, states, pltpu.VMEM((2, groups, e, e), F32), one,
             pltpu.VMEM((2, e, e), F32),
-            pltpu.VMEM((3, heads, rows, e), BF16),
             dma((4, heads)), dma((2,)),
             dma((2, ns)), dma((2, ns)),
             dma((2, groups)), dma((2, groups)),
             dma((2, ns)), dma((2, ns)),
-            dma((3, heads)),
         ],
         compiler_params=pltpu.CompilerParams(
-            collective_id=0, has_side_effects=True, vmem_limit_bytes=60 << 20
+            collective_id=0, has_side_effects=True, vmem_limit_bytes=36 << 20
         ),
     )(queries, key_rows, value_rows, out_grad, prefix_state, suffix_state)
+    out = jax.ShapeDtypeStruct((rows, heads * e), BF16)
+    return pl.pallas_call(
+        functools.partial(closing_kernel, factor),
+        out_shape=(out, out, out),
+        in_specs=[vmem] * 6,
+        out_specs=(hbm, hbm, hbm),
+        scratch_shapes=[narrow, narrow, dma((3, heads))],
+        compiler_params=pltpu.CompilerParams(vmem_limit_bytes=6 << 20),
+    )(*kept)
 
 
 def solution(mesh):

time: 75.9 us -> 72.6 us (0.957)
  local copies, waits for them, and re-layouts: 6.98 us -> 0 us
  Pallas kernels: 68.1 us -> 71.8 us
    unnamed x7 -> x0, local copies, waits for them, and re-layouts: 6.98 us -> none
    pallas_call x1 -> x2, Pallas kernels: 68.1 us -> 71.8 us  [the longest x1 64.7 us: shards(): pl.pallas_call(functools.partial(kernel, axes, factor), out_shape=(pair,...]
where the time goes in v2:
time: 72.6 us; the launch traced here: 72.5 us
  Pallas kernels  71.8 us (99%)
    pallas_call x1, Pallas kernels, shards(): pl.pallas_call(functools.partial(kernel, axes, factor), out_shape=(pair,...  64.7 us
    pallas_call x1, Pallas kernels, shards(): pl.pallas_call(functools.partial(closing_kernel, factor), out_shape=(out,...  7.16 us

profile of v2, /device:TPU:1, one launch (start us, length us, event | category | flops | bytes accessed | tf_op | source)
XLA Modules:
  0.0 72.5 jit_solution(4759066578673395616)
XLA Ops:
  0.6 64.7 %shard_map.85 = (bf16[16,512,256]{2,1,0:T(8,128)(2,1)S(1)}, bf16[16,512,256]{2,1,0:T(8,128)(2,1)S(1)}, f32[16,512,128]{2,1,0:T(8,128)S(1)}, f32[16,512,128]{2,1,...) custom-call(f32[512,2048]{1,0:T(8,128)} %q_hbm.1, f32[512,2048]{1,0:T(8,128)} %k_hbm.1, ...), custom_call_target="tpu_custom_call" | custom-call | tf_op jit(solution)/shard_map/pallas_call | solution.py:352
  65.3 7.2 %shard_map.86 = (bf16[512,2048]{1,0:T(8,128)(2,1)}, bf16[512,2048]{1,0:T(8,128)(2,1)}, bf16[512,2048]{1,0:T(8,128)(2,1)}) custom-call(bf16[16,512,256]{2,1,0:T(8,128)(2,1)S(1)} %get-tuple-element.9.k2, bf16[16,512,256]{2,1,0:T(8,128)(2,1)S(1)} %get-tuple-element.10.v2, f32[16,512,128]{2,1,0:T(8,128)S(1)} %get-tuple-element.11.acc_k, ...), custom_call_target="tpu_custom_call" | custom-call | tf_op jit(solution)/shard_map/pallas_call | solution.py:371

commit v3 on v2

--- a/solution.py
+++ b/solution.py
@@ -61,9 +61,9 @@
 def kernel(
     axes, factor,
     q_hbm, k_hbm, v_hbm, g_hbm, prefix_hbm, suffix_hbm,
-    k2, v2, acc_k, acc_v, after, qg,
-    q2, g2, qt, gt, acc_q, land_q,
-    local, gathered, totals, before, ends,
+    qg, kg, vg,
+    q2, k2, v2, g2, qt, gt, acc_q, acc_k, acc_v, land_q,
+    local, gathered, totals, before, after, ends,
     load_sem, end_sem, in_send, in_recv, tot_send, tot_recv, out_send, out_recv,
 ):
     nx, nc, ns = axes
@@ -294,7 +294,10 @@
 
     @pl.loop(0, heads)
     def _(i):
-        arrived(1, i)
+        h = arrived(1, i)
+        state = after[h]
+        kg[h] = finish(factor, v2[h], acc_k[h], state)
+        vg[h] = finish(factor, k2[h], acc_v[h], state.T)
 
     for w in range(2):
         @pl.loop(1, ns)
@@ -309,29 +312,17 @@
             total_copy(w, group, lax.rem(group + i, groups)).wait_send()
 
 
-def closing_kernel(
-    factor, k2, v2, acc_k, acc_v, after, qg, qg_hbm, kg_hbm, vg_hbm, kg, vg, store_sem
-):
+def store_kernel(qg, kg, vg, qg_hbm, kg_hbm, vg_hbm, store_sem):
     heads, _, e = qg.shape
-
-    def store(o, h):
-        src, dst = ((qg, qg_hbm), (kg, kg_hbm), (vg, vg_hbm))[o]
-        return pltpu.make_async_copy(
-            src.at[h], dst.at[:, pl.ds(pl.multiple_of(h * e, e), e)], store_sem.at[o, h]
-        )
-
-    @pl.loop(0, heads)
-    def _(h):
-        state = after[h]
-        kg[h] = finish(factor, v2[h], acc_k[h], state)
-        vg[h] = finish(factor, k2[h], acc_v[h], state.T)
-        for o in range(3):
-            store(o, h).start()
-
-    @pl.loop(0, heads)
-    def _(h):
-        for o in range(3):
-            store(o, h).wait()
+    copies = [
+        pltpu.make_async_copy(src.at[h], dst.at[:, pl.ds(h * e, e)], store_sem.at[o, h])
+        for o, (src, dst) in enumerate(((qg, qg_hbm), (kg, kg_hbm), (vg, vg_hbm)))
+        for h in range(heads)
+    ]
+    for c in copies:
+        c.start()
+    for c in copies:
+        c.wait()
 
 
 def shards(axes, queries, key_rows, value_rows, out_grad, prefix_state, suffix_state):
@@ -351,12 +342,12 @@
     narrow = pltpu.VMEM((heads, rows, e), BF16)
     kept = pl.pallas_call(
         functools.partial(kernel, axes, factor),
-        out_shape=(pair, pair, wide, wide, one, narrow),
+        out_shape=(narrow,) * 3,
         in_specs=[hbm] * 6,
-        out_specs=(vmem,) * 6,
+        out_specs=(vmem,) * 3,
         scratch_shapes=[
-            pair, pair, pair_t, pair_t, wide, wide,
-            states, states, pltpu.VMEM((2, groups, e, e), F32), one,
+            pair, pair, pair, pair, pair_t, pair_t, wide, wide, wide, wide,
+            states, states, pltpu.VMEM((2, groups, e, e), F32), one, one,
             pltpu.VMEM((2, e, e), F32),
             dma((4, heads)), dma((2,)),
             dma((2, ns)), dma((2, ns)),
@@ -364,17 +355,17 @@
             dma((2, ns)), dma((2, ns)),
         ],
         compiler_params=pltpu.CompilerParams(
-            collective_id=0, has_side_effects=True, vmem_limit_bytes=36 << 20
+            collective_id=0, has_side_effects=True, vmem_limit_bytes=52 << 20
         ),
     )(queries, key_rows, value_rows, out_grad, prefix_state, suffix_state)
     out = jax.ShapeDtypeStruct((rows, heads * e), BF16)
     return pl.pallas_call(
-        functools.partial(closing_kernel, factor),
+        store_kernel,
         out_shape=(out, out, out),
-        in_specs=[vmem] * 6,
+        in_specs=[vmem] * 3,
         out_specs=(hbm, hbm, hbm),
-        scratch_shapes=[narrow, narrow, dma((3, heads))],
-        compiler_params=pltpu.CompilerParams(vmem_limit_bytes=6 << 20),
+        scratch_shapes=[dma((3, heads))],
+        compiler_params=pltpu.CompilerParams(vmem_limit_bytes=2 << 20),
     )(*kept)
 
 

time: 72.6 us -> 68.9 us (0.949)
  Pallas kernels: 71.8 us -> 67.9 us
    pallas_call x2, Pallas kernels: 71.8 us -> 67.9 us  [the longest x1 64.8 us: shards(): pl.pallas_call(functools.partial(kernel, axes, factor), out_shape=(narrow...]
where the time goes in v3:
time: 68.9 us; the launch traced here: 68.5 us
  Pallas kernels  67.9 us (99%)
    pallas_call x1, Pallas kernels, shards(): pl.pallas_call(functools.partial(kernel, axes, factor), out_shape=(narrow...  64.8 us
    pallas_call x1, Pallas kernels, shards(): pl.pallas_call(store_kernel, out_shape=(out, out, out), in_specs=[vmem] *...  3.04 us

profile of v3, /device:TPU:1, one launch (start us, length us, event | category | flops | bytes accessed | tf_op | source)
XLA Modules:
  0.0 68.5 jit_solution(12308064264990839678)
XLA Ops:
  0.6 64.8 %shard_map.85 = (bf16[16,512,128]{2,1,0:T(8,128)(2,1)S(1)}, bf16[16,512,128]{2,1,0:T(8,128)(2,1)S(1)}, bf16[16,512,128]{2,1,0:T(8,128)(2,1)S(1)}) custom-call(f32[512,2048]{1,0:T(8,128)} %q_hbm.1, f32[512,2048]{1,0:T(8,128)} %k_hbm.1, f32[512,2048]{1,0:T(8,128)} %v_hbm.1, f32[512,2048]{1,0:T(8,128)} %g_hbm.1, f32[16,128,128]{2,1,0:T(8,128)} %prefix_hbm.1, ...), custom_call_target="tpu_custom_call" | custom-call | tf_op jit(solution)/shard_map/pallas_call | solution.py:343
  65.5 3.0 %shard_map.86 = (bf16[512,2048]{1,0:T(8,128)(2,1)}, bf16[512,2048]{1,0:T(8,128)(2,1)}, bf16[512,2048]{1,0:T(8,128)(2,1)}) custom-call(bf16[16,512,128]{2,1,0:T(8,128)(2,1)S(1)} %get-tuple-element.6.qg, bf16[16,512,128]{2,1,0:T(8,128)(2,1)S(1)} %get-tuple-element.7.kg, bf16[16,512,128]{2,1,0:T(8,128)(2,1)S(1)} %get-tuple-element.8.vg), custom_call_target="tpu_custom_call" | custom-call | tf_op jit(solution)/shard_map/pallas_call | solution.py:362

commit v4 on v3

--- a/solution.py
+++ b/solution.py
@@ -91,11 +91,20 @@
     def head_at(i):
         return lax.rem(sc + 1 + i, ns)
 
-    for pair in ((0, 1), (2, 3)):
-        @pl.loop(0, heads)
-        def _(i):
-            for a in pair:
-                load(a, head_at(i)).start()
+    barrier = pltpu.get_barrier_semaphore()
+
+    @pl.loop(1, ns)
+    def _(i):
+        pl.semaphore_signal(barrier, inc=1, device_id=peer(lax.rem(sc + i, ns)), device_id_type=MESH)
+
+    @pl.loop(1, groups)
+    def _(i):
+        pl.semaphore_signal(barrier, inc=1, device_id=group_peer(lax.rem(group + i, groups)), device_id_type=MESH)
+
+    @pl.loop(0, heads)
+    def _(i):
+        for a in (0, 1):
+            load(a, head_at(i)).start()
 
     end_copies = [
         pltpu.make_async_copy(prefix_hbm.at[sc], ends.at[0], end_sem.at[0]),
@@ -104,16 +113,6 @@
     for c in end_copies:
         c.start()
 
-    barrier = pltpu.get_barrier_semaphore()
-
-    @pl.loop(1, ns)
-    def _(i):
-        pl.semaphore_signal(barrier, inc=1, device_id=peer(lax.rem(sc + i, ns)), device_id_type=MESH)
-
-    @pl.loop(1, groups)
-    def _(i):
-        pl.semaphore_signal(barrier, inc=1, device_id=group_peer(lax.rem(group + i, groups)), device_id_type=MESH)
-
     pl.semaphore_wait(barrier, ns - 1 + groups - 1)
 
     def in_copy(w, head, source, target):
@@ -142,6 +141,9 @@
         def _(i):
             h = head_at(i)
             a, b = left, right
+            if w == 0:
+                for later in (2, 3):
+                    load(later, h).start()
             load(a, h).wait()
             load(b, h).wait()
             x2 = split2(landing[a][1][h])

time: 68.9 us -> 68.5 us (level)
  no operation moved by 1% of the time
where the time goes in v4:
time: 68.5 us; the launch traced here: 68.2 us
  Pallas kernels  67.6 us (99%)
    pallas_call x1, Pallas kernels, shards(): pl.pallas_call(functools.partial(kernel, axes, factor), out_shape=(narrow...  64.6 us
    pallas_call x1, Pallas kernels, shards(): pl.pallas_call(store_kernel, out_shape=(out, out, out), in_specs=[vmem] *...  3.04 us

profile of v4, /device:TPU:1, one launch (start us, length us, event | category | flops | bytes accessed | tf_op | source)
XLA Modules:
  0.0 68.2 jit_solution(8888492418829958710)
XLA Ops:
  0.6 64.6 %shard_map.85 = (bf16[16,512,128]{2,1,0:T(8,128)(2,1)S(1)}, bf16[16,512,128]{2,1,0:T(8,128)(2,1)S(1)}, bf16[16,512,128]{2,1,0:T(8,128)(2,1)S(1)}) custom-call(f32[512,2048]{1,0:T(8,128)} %q_hbm.1, f32[512,2048]{1,0:T(8,128)} %k_hbm.1, f32[512,2048]{1,0:T(8,128)} %v_hbm.1, f32[512,2048]{1,0:T(8,128)} %g_hbm.1, f32[16,128,128]{2,1,0:T(8,128)} %prefix_hbm.1, ...), custom_call_target="tpu_custom_call" | custom-call | tf_op jit(solution)/shard_map/pallas_call | solution.py:345
  65.2 3.0 %shard_map.86 = (bf16[512,2048]{1,0:T(8,128)(2,1)}, bf16[512,2048]{1,0:T(8,128)(2,1)}, bf16[512,2048]{1,0:T(8,128)(2,1)}) custom-call(bf16[16,512,128]{2,1,0:T(8,128)(2,1)S(1)} %get-tuple-element.6.qg, bf16[16,512,128]{2,1,0:T(8,128)(2,1)S(1)} %get-tuple-element.7.kg, bf16[16,512,128]{2,1,0:T(8,128)(2,1)S(1)} %get-tuple-element.8.vg), custom_call_target="tpu_custom_call" | custom-call | tf_op jit(solution)/shard_map/pallas_call | solution.py:364

commit v5 on v3

--- a/solution.py
+++ b/solution.py
@@ -11,7 +11,7 @@
 MESH = pl.DeviceIdType.MESH
 F32 = jnp.float32
 BF16 = jnp.bfloat16
-SEGMENTS = (1, 2, 6, 1, 6)
+SEGMENTS = (0, 2, 6, 1, 6)
 
 
 def split2(x):

time: 68.9 us -> 68.7 us (level)
  no operation moved by 1% of the time
where the time goes in v5:
time: 68.7 us; the launch traced here: 68.6 us
  Pallas kernels  68 us (99%)
    pallas_call x1, Pallas kernels, shards(): pl.pallas_call(functools.partial(kernel, axes, factor), out_shape=(narrow...  64.9 us
    pallas_call x1, Pallas kernels, shards(): pl.pallas_call(store_kernel, out_shape=(out, out, out), in_specs=[vmem] *...  3.04 us

profile of v5, /device:TPU:1, one launch (start us, length us, event | category | flops | bytes accessed | tf_op | source)
XLA Modules:
  0.0 68.6 jit_solution(7815478783762081380)
XLA Ops:
  0.6 64.9 %shard_map.85 = (bf16[16,512,128]{2,1,0:T(8,128)(2,1)S(1)}, bf16[16,512,128]{2,1,0:T(8,128)(2,1)S(1)}, bf16[16,512,128]{2,1,0:T(8,128)(2,1)S(1)}) custom-call(f32[512,2048]{1,0:T(8,128)} %q_hbm.1, f32[512,2048]{1,0:T(8,128)} %k_hbm.1, f32[512,2048]{1,0:T(8,128)} %v_hbm.1, f32[512,2048]{1,0:T(8,128)} %g_hbm.1, f32[16,128,128]{2,1,0:T(8,128)} %prefix_hbm.1, ...), custom_call_target="tpu_custom_call" | custom-call | tf_op jit(solution)/shard_map/pallas_call | solution.py:343
  65.6 3.0 %shard_map.86 = (bf16[512,2048]{1,0:T(8,128)(2,1)}, bf16[512,2048]{1,0:T(8,128)(2,1)}, bf16[512,2048]{1,0:T(8,128)(2,1)}) custom-call(bf16[16,512,128]{2,1,0:T(8,128)(2,1)S(1)} %get-tuple-element.6.qg, bf16[16,512,128]{2,1,0:T(8,128)(2,1)S(1)} %get-tuple-element.7.kg, bf16[16,512,128]{2,1,0:T(8,128)(2,1)S(1)} %get-tuple-element.8.vg), custom_call_target="tpu_custom_call" | custom-call | tf_op jit(solution)/shard_map/pallas_call | solution.py:362
